TPU v7x, 32 devices: a whole 2x2x4 slice. The times are simulated.
32 devices in a mesh: gx: 4 (over z), yz: 8 (over y, x, core).
Axes of the slice: x: 2, y: 2, z: 4, core: 2. Of those that a mesh axis runs over, the one named last changes fastest.
Arguments:
- positions: bfloat16 [3, 8192], P(None, ('gx', 'yz')), may hold values from 0 to 1
- species: int32 [8192], P(('gx', 'yz')), may hold values from 0 to 5
- features: bfloat16 [8192, 512], P(('gx', 'yz')), may hold values from -6 to 6
- move_dest: int32 [64], P(('gx', 'yz')), may hold values from 0 to 7, as said below
- move_slot: int32 [64], P(('gx', 'yz')), may hold values from 0 to 1, as said below
- halo_list: int32 [1024], P(('gx', 'yz')), may hold values from 0 to 255
- neighbours: int32 [8192, 64], P(('gx', 'yz')), may hold values from 0 to 383, as said below
- neighbour_count: int32 [8192], P(('gx', 'yz')), may hold values from 16 to 64
- wave_index: int32 [3, 4096], replicated, may hold values from -16 to 16, as said below
- radial_in: bfloat16 [8, 64], replicated, may hold values from -2 to 2
- radial_mid: bfloat16 [2, 64, 64], replicated, may hold values from -0.75 to 0.75
- radial_out: bfloat16 [64, 512], replicated, may hold values from -0.75 to 0.75
- up_weight: bfloat16 [2, 128, 128], replicated, may hold values from -0.5 to 0.5
- prod_weight: float32 [6, 640], replicated, may hold values from -4 to 4
- out_weight: bfloat16 [2, 128, 128], replicated, may hold values from -0.5 to 0.5
- skip_weight: bfloat16 [2, 128, 128], replicated, may hold values from -0.5 to 0.5
- charge_weight: bfloat16 [128, 8], replicated, may hold values from -0.5 to 0.5
- field_weight: float32 [8, 128], replicated, may hold values from -2 to 2
- read_weight: bfloat16 [128, 16], replicated, may hold values from -0.5 to 0.5
- read_vector: float32 [16], replicated, may hold values from -1.5 to 1.5
- force_weight: float32 [128], replicated, may hold values from -0.5 to 0.5
Outputs:
- forces: float32 [3, 8192], P(None, ('gx', 'yz'))
- energies: float32 [8192], P(('gx', 'yz'))
Inputs may be any that keep to these rules, and one draw needn't show every extreme that they name: `move_dest`: the destination lies in the same gx row. Exactly 2 blocks of each device go to other devices, at most one to any one device, and each device receives exactly 2 blocks; the others stay. `move_slot`: the 2 blocks that a device holds after the move take its 2 slots once each. `neighbours`: row of the device's table: its working atoms, then the ghosts from gx - 1, gx + 1, yz - 1, yz + 1. Never the atom itself; slots from neighbour_count on are padding. `wave_index`: row 0 runs from 1 to 8, row 1 from -16 to 16, row 2 from -2 to 2.
All inputs are finite; a program needn't handle non-finite values.
Results may differ from a plain program's by a relative error of at most 0.0028.
Values may be sent and summed in bfloat16 or wider, within the bound.
A program may use at most 64 MiB of HBM per device.

v0:
```python
import math

import jax
import jax.numpy as jnp
from jax import lax
from jax.sharding import PartitionSpec as P

highest = lax.Precision.HIGHEST
two_pi = 2.0 * math.pi
cutoff_radius = 3.5
basis_sharpness = 4.0
ewald_width = 0.1
ewald_scale = 0.01
atom_step = 64
wave_step = 512


def with_halo(value, sides, width):
    for axis, dim in sides:
        count, length = (lax.axis_size(axis), value.shape[dim])
        up = [(i, (i + 1) % count) for i in range(count)]
        down = [(j, i) for i, j in up]
        last = lax.slice_in_dim(value, length - width, length, axis=dim)
        leading = lax.slice_in_dim(value, 0, width, axis=dim)
        before = lax.ppermute(last, axis, up)
        after = lax.ppermute(leading, axis, down)
        value = jnp.concatenate([before, value, after], axis=dim)
    return value


def wave_vectors(wave_index, domains_x, domains_y):
    scales = jnp.array([two_pi / domains_x, two_pi / domains_y, two_pi], jnp.float32)
    wavevectors = wave_index.astype(jnp.float32) * scales[:, None]
    squared = jnp.sum(wavevectors * wavevectors, axis=0)
    prefactor = 8.0 * math.pi * ewald_scale / (domains_x * domains_y)
    weights = prefactor * jnp.exp(-0.5 * ewald_width * ewald_width * squared) / squared
    return (wavevectors, weights)


def phase_of(absolute, wavevectors):
    return (
        absolute[0][:, None] * wavevectors[0][None, :]
        + absolute[1][:, None] * wavevectors[1][None, :]
        + absolute[2][:, None] * wavevectors[2][None, :]
    )


def structure_terms(absolute, charges, wavevectors):
    stride = math.gcd(wavevectors.shape[1], wave_step)
    block_count = wavevectors.shape[1] // stride

    def one_block(block_index):
        wave_block = lax.dynamic_slice_in_dim(wavevectors, block_index * stride, stride, 1)
        phases = phase_of(absolute, wave_block)
        real_part = jnp.einsum("ak,aq->kq", jnp.cos(phases), charges, precision=highest)
        imag_part = jnp.einsum("ak,aq->kq", jnp.sin(phases), charges, precision=highest)
        return (real_part, imag_part)

    real_part, imag_part = lax.map(one_block, jnp.arange(block_count, dtype=jnp.int32))
    latent = charges.shape[1]
    return (real_part.reshape(-1, latent), imag_part.reshape(-1, latent))


def field_terms(absolute, wavevectors, weights, total_real, total_imag):
    scaled_real = weights[:, None] * total_real
    scaled_imag = weights[:, None] * total_imag
    right_cos = jnp.concatenate(
        [scaled_real] + [-wavevectors[direction][:, None] * scaled_imag for direction in range(3)],
        axis=1,
    )
    right_sin = jnp.concatenate(
        [scaled_imag] + [wavevectors[direction][:, None] * scaled_real for direction in range(3)],
        axis=1,
    )
    stride = math.gcd(wavevectors.shape[1], wave_step)
    block_count = wavevectors.shape[1] // stride

    def accumulate(block_index, running):
        wave_block = lax.dynamic_slice_in_dim(wavevectors, block_index * stride, stride, 1)
        phases = phase_of(absolute, wave_block)
        cos_right = lax.dynamic_slice_in_dim(right_cos, block_index * stride, stride, 0)
        sin_right = lax.dynamic_slice_in_dim(right_sin, block_index * stride, stride, 0)
        running = running + jnp.dot(jnp.cos(phases), cos_right, precision=highest)
        return running + jnp.dot(jnp.sin(phases), sin_right, precision=highest)

    initial = jnp.zeros((absolute.shape[1], right_cos.shape[1]), jnp.float32)
    return lax.fori_loop(0, block_count, accumulate, initial)


def project_pair(feature, weights):
    channels = weights.shape[1]
    row_count = feature.shape[0]
    scalar = jnp.dot(feature[:, :channels], weights[0], preferred_element_type=jnp.float32)
    vector = jnp.dot(
        feature[:, channels:].reshape(row_count * 3, channels),
        weights[1],
        preferred_element_type=jnp.float32,
    )
    return jnp.concatenate([scalar, vector.reshape(row_count, 3 * channels)], axis=1)


def edge_products(
    table_pos, table_up, centre_pos, nbr_rows, nbr_live, coeffs, radial_in, radial_mid, radial_out
):
    atom_count, slot_count = nbr_rows.shape
    edge_count = atom_count * slot_count
    table_size = table_up.shape[0]
    flat_rows = nbr_rows.reshape(edge_count)
    row_onehot = (flat_rows[:, None] == jnp.arange(table_size, dtype=jnp.int32)[None, :]).astype(
        jnp.bfloat16
    )
    picked_pos = jnp.dot(row_onehot.astype(jnp.float32), table_pos.T, precision=highest)
    offset = (picked_pos.T.reshape(3, atom_count, slot_count) - centre_pos[:, :, None]).reshape(
        3, edge_count
    )
    distance = jnp.sqrt(jnp.sum(offset * offset, axis=0))
    scaled_dist = distance / cutoff_radius
    envelope = 1.0 - 28.0 * scaled_dist**6 + 48.0 * scaled_dist**7 - 21.0 * scaled_dist**8
    alive_mask = (
        (jnp.arange(slot_count, dtype=jnp.int32)[None, :] < nbr_live[:, None])
        .astype(jnp.float32)
        .reshape(edge_count)
    )
    basis_count = radial_in.shape[0]
    centres = jnp.arange(basis_count, dtype=jnp.float32) * (cutoff_radius / (basis_count - 1))
    radial_basis = jnp.exp(-basis_sharpness * (distance[:, None] - centres[None, :]) ** 2).astype(
        jnp.bfloat16
    )
    hidden = jax.nn.silu(
        jnp.dot(radial_basis, radial_in, preferred_element_type=jnp.float32)
    ).astype(jnp.bfloat16)
    hidden = jax.nn.silu(jnp.dot(hidden, radial_mid[0], preferred_element_type=jnp.float32)).astype(
        jnp.bfloat16
    )
    hidden = jax.nn.silu(jnp.dot(hidden, radial_mid[1], preferred_element_type=jnp.float32)).astype(
        jnp.bfloat16
    )
    radial = (
        jnp.dot(hidden, radial_out, preferred_element_type=jnp.float32)
        * (envelope * alive_mask)[:, None]
    ).astype(jnp.bfloat16)
    channels = radial.shape[1] // 4
    gathered = jnp.dot(row_onehot, table_up, preferred_element_type=jnp.float32)

    def column_block(source, number):
        return source[:, number * channels : (number + 1) * channels].astype(jnp.float32)

    norm_factor = 1.0 / math.sqrt(slot_count)

    def neighbour_sum(values):
        return jnp.sum(values.reshape(atom_count, slot_count, channels), axis=1) * norm_factor

    up_scalar = column_block(gathered, 0)
    up_vector = [column_block(gathered, 1 + direction) for direction in range(3)]
    along = (
        up_vector[0] * offset[0][:, None]
        + up_vector[1] * offset[1][:, None]
        + up_vector[2] * offset[2][:, None]
    )
    scalar_msg = neighbour_sum(
        column_block(radial, 0) * up_scalar + column_block(radial, 1) * along
    )
    radial_scalar = column_block(radial, 2) * up_scalar
    radial_vector = column_block(radial, 3)
    vector_msg = [
        neighbour_sum(
            radial_scalar * offset[direction][:, None] + radial_vector * up_vector[direction]
        )
        for direction in range(3)
    ]
    square_sum = (
        vector_msg[0] * vector_msg[0]
        + vector_msg[1] * vector_msg[1]
        + vector_msg[2] * vector_msg[2]
    )
    path_weights = [coeffs[:, number * channels : (number + 1) * channels] for number in range(5)]
    scalar_prod = (
        path_weights[0] * scalar_msg
        + path_weights[1] * scalar_msg * scalar_msg
        + path_weights[2] * square_sum
    )
    vector_prod = [
        path_weights[3] * vector_msg[direction]
        + path_weights[4] * scalar_msg * vector_msg[direction]
        for direction in range(3)
    ]
    return jnp.concatenate([scalar_prod] + vector_prod, axis=1).astype(jnp.bfloat16)


def atom_results(
    work_feat,
    products,
    charges,
    efield,
    out_weight,
    skip_weight,
    field_weight,
    read_weight,
    read_vector,
    force_weight,
):
    channels = out_weight.shape[1]
    latent = charges.shape[1]
    mixed_feat = project_pair(products, out_weight) + project_pair(work_feat, skip_weight)
    potential = efield[:, :latent]
    scalars = mixed_feat[:, :channels] + jnp.dot(potential, field_weight, precision=highest)
    readout = jax.nn.silu(
        jnp.dot(scalars.astype(jnp.bfloat16), read_weight, preferred_element_type=jnp.float32)
    )
    energy = jnp.dot(readout, read_vector, precision=highest) + 0.5 * jnp.sum(
        charges * potential, axis=1
    )
    forces = [
        jnp.dot(
            mixed_feat[:, (1 + direction) * channels : (2 + direction) * channels],
            force_weight,
            precision=highest,
        )
        + jnp.sum(charges * efield[:, (1 + direction) * latent : (2 + direction) * latent], axis=1)
        for direction in range(3)
    ]
    return jnp.stack(forces + [energy])


def pick_float(chosen, source):
    return jnp.einsum("ab,bij->aij", chosen, source, precision=highest)


def pick_half(chosen, source):
    return jnp.einsum(
        "ab,bij->aij", chosen.astype(jnp.bfloat16), source, preferred_element_type=jnp.float32
    )


def on_device(
    positions,
    species,
    features,
    move_dest,
    move_slot,
    halo_list,
    neighbours,
    neighbour_count,
    wave_index,
    radial_in,
    radial_mid,
    radial_out,
    up_weight,
    prod_weight,
    out_weight,
    skip_weight,
    charge_weight,
    field_weight,
    read_weight,
    read_vector,
    force_weight,
):
    blocks = move_dest.shape[0]
    atom_count = positions.shape[1]
    block_size = atom_count // blocks
    channels = up_weight.shape[1]
    domains_x = lax.axis_size("gx")
    domains_y = lax.axis_size("yz")
    column = lax.axis_index("yz")
    layer_row = lax.axis_index("gx")
    column_f = column.astype(jnp.float32)
    slot_iota = jnp.arange(blocks, dtype=jnp.int32)
    slot_float = slot_iota.astype(jnp.float32)
    peer_iota = jnp.arange(domains_y, dtype=jnp.int32)
    moving = move_dest != column
    meta_rows = jnp.stack(
        [
            move_slot.astype(jnp.float32) + 1.0,
            slot_float,
            jnp.zeros((blocks,), jnp.float32) + column_f + 1.0,
            move_dest.astype(jnp.float32) + 1.0,
        ],
        axis=1,
    )
    home_geo = jnp.concatenate(
        [
            positions.reshape(3, blocks, block_size).transpose(1, 0, 2),
            species.astype(jnp.bfloat16).reshape(blocks, 1, block_size),
            jnp.broadcast_to(meta_rows[:, :, None], (blocks, 4, block_size)).astype(jnp.bfloat16),
        ],
        axis=1,
    )
    home_feat = features.reshape(blocks, block_size, 4 * channels)
    stay_pick = ((move_slot[None, :] == slot_iota[:, None]) & ~moving[None, :]).astype(jnp.float32)
    send_pick = ((move_dest[None, :] == peer_iota[:, None]) & moving[None, :]).astype(jnp.float32)
    out_geo = pick_half(send_pick, home_geo).astype(jnp.bfloat16)
    out_feat = pick_half(send_pick, home_feat).astype(jnp.bfloat16)
    in_geo, in_feat = (
        lax.all_to_all(out_geo, "yz", split_axis=0, concat_axis=0, tiled=True),
        lax.all_to_all(out_feat, "yz", split_axis=0, concat_axis=0, tiled=True),
    )
    arrive_pick = (
        in_geo[:, 4, 0].astype(jnp.float32)[None, :] == slot_float[:, None] + 1.0
    ).astype(jnp.float32)
    arrive_geo = pick_half(arrive_pick, in_geo)
    arrive_feat = pick_half(arrive_pick, in_feat)
    work_geo = pick_half(stay_pick, home_geo) + arrive_geo
    work_feat = (
        (pick_half(stay_pick, home_feat) + arrive_feat)
        .astype(jnp.bfloat16)
        .reshape(atom_count, 4 * channels)
    )
    work_pos = work_geo[:, :3].transpose(1, 0, 2).reshape(3, atom_count)
    work_species = work_geo[:, 3].reshape(atom_count)
    home_of_slot = work_geo[:, 6, 0] - 1.0
    arrived = home_of_slot != column_f
    list_pick = (halo_list[:, None] == jnp.arange(atom_count, dtype=jnp.int32)[None, :]).astype(
        jnp.float32
    )
    send_pos = jnp.dot(work_pos, list_pick.T, precision=highest).astype(jnp.bfloat16)
    send_feat = jnp.dot(
        list_pick.astype(jnp.bfloat16), work_feat, preferred_element_type=jnp.float32
    ).astype(jnp.bfloat16)
    ext_pos, ext_feat = (
        with_halo(send_pos[None, None], (("gx", 0), ("yz", 1)), 1),
        with_halo(send_feat[None, None], (("gx", 0), ("yz", 1)), 1),
    )
    unit_axes = jnp.eye(3, dtype=jnp.float32)
    ghost_pos = [
        ext_pos[0, 1].astype(jnp.float32) - unit_axes[0][:, None],
        ext_pos[2, 1].astype(jnp.float32) + unit_axes[0][:, None],
        ext_pos[1, 0].astype(jnp.float32) - unit_axes[1][:, None],
        ext_pos[1, 2].astype(jnp.float32) + unit_axes[1][:, None],
    ]
    table_pos = jnp.concatenate([work_pos] + ghost_pos, axis=1)
    table_feat = jnp.concatenate(
        [work_feat, ext_feat[0, 1], ext_feat[2, 1], ext_feat[1, 0], ext_feat[1, 2]], axis=0
    )
    anchor = jnp.stack([layer_row.astype(jnp.float32), column_f, jnp.zeros((), jnp.float32)])
    absolute = work_pos + anchor[:, None]
    charges = jnp.dot(work_feat[:, :channels], charge_weight, preferred_element_type=jnp.float32)
    wavevectors, weights = wave_vectors(wave_index, domains_x, domains_y)
    part_real, part_imag = structure_terms(absolute, charges, wavevectors)
    total_real, total_imag = lax.psum((part_real, part_imag), ("gx", "yz"))
    table_up = project_pair(table_feat, up_weight).astype(jnp.bfloat16)
    onehot = (
        work_species[:, None] == jnp.arange(prod_weight.shape[0], dtype=jnp.float32)[None, :]
    ).astype(jnp.float32)
    coeffs = jnp.dot(onehot, prod_weight, precision=highest)
    block_count = atom_count // atom_step

    def edge_block(pieces):
        return edge_products(
            table_pos,
            table_up,
            pieces[2],
            pieces[0],
            pieces[1],
            pieces[3],
            radial_in,
            radial_mid,
            radial_out,
        )

    products = lax.map(
        edge_block,
        (
            neighbours.reshape(block_count, atom_step, -1),
            neighbour_count.reshape(block_count, atom_step),
            work_pos.reshape(3, block_count, atom_step).transpose(1, 0, 2),
            coeffs.reshape(block_count, atom_step, -1),
        ),
    ).reshape(atom_count, 4 * channels)
    efield = field_terms(absolute, wavevectors, weights, total_real, total_imag)
    results = atom_results(
        work_feat,
        products,
        charges,
        efield,
        out_weight,
        skip_weight,
        field_weight,
        read_weight,
        read_vector,
        force_weight,
    )
    res_blocks = results.reshape(4, blocks, block_size).transpose(1, 0, 2)
    back_pick = (
        (home_of_slot[None, :] == peer_iota.astype(jnp.float32)[:, None]) & arrived[None, :]
    ).astype(jnp.float32)
    sent_back = pick_float(back_pick, res_blocks)
    came_back = lax.all_to_all(sent_back, "yz", split_axis=0, concat_axis=0, tiled=True)
    remote_pick = ((move_dest[:, None] == peer_iota[None, :]) & moving[:, None]).astype(jnp.float32)
    remote = pick_float(remote_pick, came_back)
    home_res = pick_float(stay_pick.T, res_blocks) + remote
    flat_res = home_res.transpose(1, 0, 2).reshape(4, atom_count)
    return (flat_res[:3], flat_res[3])


def solution(mesh):
    in_specs = (
        P(None, ("gx", "yz")),
        P(("gx", "yz")),
        P(("gx", "yz"), None),
        P(("gx", "yz")),
        P(("gx", "yz")),
        P(("gx", "yz")),
        P(("gx", "yz"), None),
        P(("gx", "yz")),
        P(),
        P(),
        P(),
        P(),
        P(),
        P(),
        P(),
        P(),
        P(),
        P(),
        P(),
        P(),
        P(),
    )
    out_specs = (P(None, ("gx", "yz")), P(("gx", "yz")))
    return jax.shard_map(
        on_device, mesh=mesh, in_specs=in_specs, out_specs=out_specs, check_vma=False
    )
```

profile of v0, /device:TPU:0, one launch (start us, length us, event | category | flops | bytes accessed | tf_op | source)
XLA Modules:
  0.0 382.4 jit_solution(8578587456457187002)
XLA Ops:
  12.4 5.2 %all-to-all-start = ((bf16[8,8,128]{2,1,0:T(8,128)(2,1)}), bf16[8,8,128]{2,1,0:T(8,128)(2,1)S(1)}, u32[]{:S(2)}, u32[]{:S(2)}) async-start(bf16[8,8,128]{2,1,0:T(8,128)(2,1)} %copy.64), calls=%async_computation | async-start | bytes 32768 | tf_op jit(solution)/shard_map/all_to_all | solution.py:294
  24.0 4.2 %all-to-all-start.1 = ((bf16[8,128,512]{2,1,0:T(8,128)(2,1)}), bf16[8,128,512]{2,1,0:T(8,128)(2,1)S(1)}, u32[]{:S(2)}, u32[]{:S(2)}) async-start(bf16[8,128,512]{2,1,0:T(8,128)(2,1)} %copy.71), calls=%async_computation.1 | async-start | bytes 2097152 | tf_op jit(solution)/shard_map/all_to_all | solution.py:295
  37.3 5.7 %collective-permute-done.2 = bf16[3,1,3,32]{3,2,1,0:T(4,128)(2,1)S(1)} collective-permute-done((bf16[3,1,3,32]{3,2,1,0:T(4,128)(2,1)S(1)}, bf16[3,1,3,32]{3,2,1,0:T(4,128)(2,1)S(1)}, u32[]{:S(2)}, u32[]{:S(2)}) %collective-permute-start.2) | collective-permute-done | bytes 608 | tf_op jit(solution)/shard_map/ppermute | solution.py:25
  49.9 56.6 %while.37 = (s32[]{:T(128)}, f32[8,512,8]{1,2,0:T(8,128)}, f32[8,512,8]{1,2,0:T(8,128)}, f32[3,256]{1,0:T(4,128)S(1)}, s32[8]{0:T(128)S(1)}, /*index=5*/f32[3,40...) while((s32[]{:T(128)}, f32[8,512,8]{1,2,0:T(8,128)}, ...), condition=%wide.region_9.10_spmd, body=%wide.region_8.9_spmd.sunk | while | flops 26476552 | bytes 87259 | solution.py:59
  51.3 2.9 fusion.239
  54.2 2.9 fusion.238
  58.4 2.9 fusion.239
  65.4 2.9 fusion.239
  72.5 2.9 fusion.239
  79.6 2.9 fusion.239
  86.7 2.9 fusion.239
  93.7 2.9 fusion.239
  96.6 2.9 fusion.238
  100.8 2.9 fusion.239
  103.7 2.9 fusion.238
  110.5 121.8 %all-reduce.3.cloned.1.call-done = (f32[4096,8]{0,1:T(8,128)}, f32[4096,8]{0,1:T(8,128)}) async-done(((f32[4096,8]{0,1:T(8,128)}, f32[4096,8]{0,1:T(8,128)}), (f32[4096,8]{0,1:T(8,128)}, f32[4096,8]{0,1:T(8,128)})) %all-reduce.3.cloned.1.call-update) | async-done | bytes 262160 | tf_op jit(solution)/shard_map/psum | solution.py:339
  233.5 54.9 %while.38 = (s32[]{:T(128)}, f32[256,32]{0,1:T(8,128)S(1)}, f32[3,256]{1,0:T(4,128)S(1)}, f32[3,4096]{1,0:T(4,128)S(1)}, f32[4096,32]{0,1:T(8,128)S(1)}, /*index...) while((s32[]{:T(128)}, f32[256,32]{0,1:T(8,128)S(1)}, ...), condition=%wide.region_13.14_spmd.clone, body=%wide.region_12.13_spmd.clone.sunk | while | flops 101998600 | bytes 299225 | solution.py:87
  234.2 3.1 convolution_add_fusion.8
  237.2 3.1 convolution_add_fusion.9
  241.0 3.1 convolution_add_fusion.8
  244.1 3.1 convolution_add_fusion.9
  247.9 3.1 convolution_add_fusion.8
  251.0 3.1 convolution_add_fusion.9
  254.8 3.1 convolution_add_fusion.8
  257.8 3.1 convolution_add_fusion.9
  261.6 3.1 convolution_add_fusion.8
  264.7 3.1 convolution_add_fusion.9
  268.5 3.1 convolution_add_fusion.8
  271.6 3.1 convolution_add_fusion.9
  275.4 3.1 convolution_add_fusion.8
  278.4 3.1 convolution_add_fusion.9
  282.2 3.1 convolution_add_fusion.8
  285.3 3.1 convolution_add_fusion.9
  291.8 70.9 %while.36 = (s32[]{:T(128)}, bf16[4,64,512]{2,1,0:T(8,128)(2,1)S(1)}, f32[4,64,640]{2,1,0:T(8,128)S(1)}, s32[4,64,64]{2,1,0:T(8,128)S(1)}, f32[3,384]{1,0:T(4,12...) while((s32[]{:T(128)}, ...), condition=%wide.region_6.7_spmd, body=%wide.region_0.6_spmd.sunk | while | flops 2032549888 | bytes 45476804 | solution.py:360
  293.0 3.1 multiply_reduce_fusion.7
  298.7 4.6 %multiply_convert_fusion.13 = bf16[4096,512]{1,0:T(8,128)(2,1)} fusion(bf16[64,512]{1,0:T(8,128)(2,1)S(1)} %get-tuple-element.587, f32[4096]{0:T(1024)S(1)} %get-tuple-element.517, bf16[4096,64]{0,1:T(8,128)(2,1)} %multiply_convert_fusion.12, bf16[2,64,64]{2,1,0:T(8,128)(2,1)S(1)} %get-tuple-element.586), kind=kOutput, calls=%fused_computation.clone.1 | convolution fusion | flops 307494912 | bytes 4816896 | tf_op jit(solution)/shard_map/while/body/eval_jaxpr/dot_general | solution.py:139
  306.1 3.4 bitcast_reduce_fusion.5
  310.6 3.1 multiply_reduce_fusion.7
  316.3 4.6 %multiply_convert_fusion.13 = bf16[4096,512]{1,0:T(8,128)(2,1)} fusion(bf16[64,512]{1,0:T(8,128)(2,1)S(1)} %get-tuple-element.587, f32[4096]{0:T(1024)S(1)} %get-tuple-element.517, bf16[4096,64]{0,1:T(8,128)(2,1)} %multiply_convert_fusion.12, bf16[2,64,64]{2,1,0:T(8,128)(2,1)S(1)} %get-tuple-element.586), kind=kOutput, calls=%fused_computation.clone.1 | convolution fusion | flops 307494912 | bytes 4816896 | tf_op jit(solution)/shard_map/while/body/eval_jaxpr/dot_general | solution.py:139
  323.8 3.4 bitcast_reduce_fusion.5
  328.3 3.1 multiply_reduce_fusion.7
  334.0 4.6 %multiply_convert_fusion.13 = bf16[4096,512]{1,0:T(8,128)(2,1)} fusion(bf16[64,512]{1,0:T(8,128)(2,1)S(1)} %get-tuple-element.587, f32[4096]{0:T(1024)S(1)} %get-tuple-element.517, bf16[4096,64]{0,1:T(8,128)(2,1)} %multiply_convert_fusion.12, bf16[2,64,64]{2,1,0:T(8,128)(2,1)S(1)} %get-tuple-element.586), kind=kOutput, calls=%fused_computation.clone.1 | convolution fusion | flops 307494912 | bytes 4816896 | tf_op jit(solution)/shard_map/while/body/eval_jaxpr/dot_general | solution.py:139
  341.5 3.4 bitcast_reduce_fusion.5
  346.0 3.1 multiply_reduce_fusion.7
  351.7 4.6 %multiply_convert_fusion.13 = bf16[4096,512]{1,0:T(8,128)(2,1)} fusion(bf16[64,512]{1,0:T(8,128)(2,1)S(1)} %get-tuple-element.587, f32[4096]{0:T(1024)S(1)} %get-tuple-element.517, bf16[4096,64]{0,1:T(8,128)(2,1)} %multiply_convert_fusion.12, bf16[2,64,64]{2,1,0:T(8,128)(2,1)S(1)} %get-tuple-element.586), kind=kOutput, calls=%fused_computation.clone.1 | convolution fusion | flops 307494912 | bytes 4816896 | tf_op jit(solution)/shard_map/while/body/eval_jaxpr/dot_general | solution.py:139
  359.1 3.4 bitcast_reduce_fusion.5
  365.8 3.6 all-to-all-start.2
  369.6 4.5 %all-to-all-done.2 = f32[8,4,128]{2,1,0:T(4,128)S(1)} async-done(((f32[8,4,128]{2,1,0:T(4,128)}), f32[8,4,128]{2,1,0:T(4,128)S(1)}, u32[]{:S(2)}, u32[]{:S(2)}) %all-to-all-start.2) | async-done | bytes 16416 | tf_op jit(solution)/shard_map/all_to_all | solution.py:387
  (320 shorter events, 91.1 us)
Async XLA Ops:
  7.2 11.3 %copy-start = (bf16[256,512]{1,0:T(8,128)(2,1)S(1)}, bf16[256,512]{1,0:T(8,128)(2,1)}, u32[]{:S(2)}) copy-start(bf16[256,512]{1,0:T(8,128)(2,1)} %param.30) | copy-start | bytes 786436
  7.2 14.4 %copy-start.18 = (f32[3]{0:T(128)S(1)}, f32[3]{0:T(128)}, u32[]{:S(2)}) copy-start(f32[3]{0:T(128)} %constant.114.clone) | copy-start | bytes 40
  7.2 14.4 %copy-start.6 = (s32[3,4096]{1,0:T(4,128)S(1)}, s32[3,4096]{1,0:T(4,128)}, u32[]{:S(2)}) copy-start(s32[3,4096]{1,0:T(4,128)} %param.36) | copy-start | bytes 147460
  8.6 14.6 %copy-start.14 = (pred[2]{0:T(512)(128)(4,1)}, pred[2]{0:T(512)(128)(4,1)S(1)}, u32[]{:S(2)}) copy-start(pred[2]{0:T(512)(128)(4,1)S(1)} %get-tuple-element.307) | copy-start | bytes 10
  8.6 14.6 %copy-start.19 = (pred[2]{0:T(512)(128)(4,1)}, pred[2]{0:T(512)(128)(4,1)S(1)}, u32[]{:S(2)}) copy-start(pred[2]{0:T(512)(128)(4,1)S(1)} %get-tuple-element.306) | copy-start | bytes 10
  12.4 11.6 %all-to-all-start = ((bf16[8,8,128]{2,1,0:T(8,128)(2,1)}), bf16[8,8,128]{2,1,0:T(8,128)(2,1)S(1)}, u32[]{:S(2)}, u32[]{:S(2)}) async-start(bf16[8,8,128]{2,1,0:T(8,128)(2,1)} %copy.64), calls=%async_computation | async-start | bytes 32768 | tf_op jit(solution)/shard_map/all_to_all | solution.py:294
  18.5 4.7 %copy-start.2 = (s32[256,64]{0,1:T(8,128)S(1)}, s32[256,64]{0,1:T(8,128)}, u32[]{:S(2)}) copy-start(s32[256,64]{0,1:T(8,128)} %param.34) | copy-start | bytes 196612
  19.8 3.6 copy-start.16
  21.9 6.7 %copy-start.17 = (s32[32]{0:T(128)S(1)}, s32[32]{0:T(128)}, u32[]{:S(2)}) copy-start(s32[32]{0:T(128)} %param.33) | copy-start | bytes 388
  21.9 11.5 %copy-start.7 = (f32[6,640]{1,0:T(8,128)S(1)}, f32[6,640]{1,0:T(8,128)}, u32[]{:S(2)}) copy-start(f32[6,640]{1,0:T(8,128)} %param.41) | copy-start | bytes 46084
  24.0 19.8 %all-to-all-start.1 = ((bf16[8,128,512]{2,1,0:T(8,128)(2,1)}), bf16[8,128,512]{2,1,0:T(8,128)(2,1)S(1)}, u32[]{:S(2)}, u32[]{:S(2)}) async-start(bf16[8,128,512]{2,1,0:T(8,128)(2,1)} %copy.71), calls=%async_computation.1 | async-start | bytes 2097152 | tf_op jit(solution)/shard_map/all_to_all | solution.py:295
  28.2 21.6 %copy-start.23 = (bf16[128,8]{0,1:T(8,128)(2,1)S(1)}, bf16[128,8]{0,1:T(8,128)(2,1)}, u32[]{:S(2)}) copy-start(bf16[128,8]{0,1:T(8,128)(2,1)} %param.44) | copy-start | bytes 6148
  28.2 204.1 %all-reduce.3.cloned.1.call-start = ((), (), s32[]{:S(2)}) async-start(), calls=%async_computation.3 | async-start | bytes 524288 | tf_op jit(solution)/shard_map/psum | solution.py:339
  28.8 5.8 %collective-permute-start = (bf16[1,1,3,32]{3,2,1,0:T(4,128)(2,1)S(1)}, bf16[1,1,3,32]{3,2,1,0:T(4,128)(2,1)S(1)}, u32[]{:S(2)}, u32[]{:S(2)}) collective-permute-start(bf16[1,1,3,32]{3,2,1,0:T(4,128)(2,1)S(1)} %fusion.86), channel_id=1, source_target_pairs={{0,8},{8,16},{16,24},{24,0},{1,9},{9,17},{17,25},{25,1},{2,10},{10... | collective-permute-start | bytes 584 | tf_op jit(solution)/shard_map/ppermute | solution.py:25
  30.3 4.2 %collective-permute-start.1 = (bf16[1,1,3,32]{3,2,1,0:T(4,128)(2,1)S(1)}, bf16[1,1,3,32]{3,2,1,0:T(4,128)(2,1)S(1)}, u32[]{:S(2)}, u32[]{:S(2)}) collective-permute-start(bf16[1,1,3,32]{3,2,1,0:T(4,128)(2,1)S(1)} %fusion.86), channel_id=1, source_target_pairs={{8,0},{16,8},{24,16},{0,24},{9,1},{17,9},{25,17},{1,25},{10,2},{18... | collective-permute-start | bytes 584 | tf_op jit(solution)/shard_map/ppermute | solution.py:26
  32.7 13.0 %copy-start.27 = (f32[2]{0:T(128)}, f32[2]{0:T(128)S(1)}, u32[]{:S(2)}) copy-start(f32[2]{0:T(128)S(1)} %fusion.147) | copy-start | bytes 28
  34.6 8.5 %collective-permute-start.2 = (bf16[3,1,3,32]{3,2,1,0:T(4,128)(2,1)S(1)}, bf16[3,1,3,32]{3,2,1,0:T(4,128)(2,1)S(1)}, u32[]{:S(2)}, u32[]{:S(2)}) collective-permute-start(bf16[3,1,3,32]{3,2,1,0:T(4,128)(2,1)S(1)} %pad_maximum_fusion.5), channel_id=1, source_target_pairs={{0,1},{1,2},{2,3},{3,4},{4,5},{5,6},{6,7},{7,0},{8,9},{9,10},{10,1... | collective-permute-start | bytes 1736 | tf_op jit(solution)/shard_map/ppermute | solution.py:25
  34.6 8.4 %collective-permute-start.3 = (bf16[3,1,3,32]{3,2,1,0:T(4,128)(2,1)S(1)}, bf16[3,1,3,32]{3,2,1,0:T(4,128)(2,1)S(1)}, u32[]{:S(2)}, u32[]{:S(2)}) collective-permute-start(bf16[3,1,3,32]{3,2,1,0:T(4,128)(2,1)S(1)} %pad_maximum_fusion.5), channel_id=1, source_target_pairs={{1,0},{2,1},{3,2},{4,3},{5,4},{6,5},{7,6},{0,7},{9,8},{10,9},{11,1... | collective-permute-start | bytes 1736 | tf_op jit(solution)/shard_map/ppermute | solution.py:26
  45.9 61.9 %collective-permute-start.4 = (bf16[1,1,32,512]{3,2,1,0:T(8,128)(2,1)S(1)}, bf16[1,1,32,512]{3,2,1,0:T(8,128)(2,1)S(1)}, u32[]{:S(2)}, u32[]{:S(2)}) collective-permute-start(bf16[1,1,32,512]{3,2,1,0:T(8,128)(2,1)S(1)} %fusion.84), channel_id=1, source_target_pairs={{0,8},{8,16},{16,24},{24,0},{1,9},{9,17},{17,25},{25,1},{2,10},{10... | collective-permute-start | bytes 98312 | tf_op jit(solution)/shard_map/ppermute | solution.py:25
  47.5 60.3 %collective-permute-start.5 = (bf16[1,1,32,512]{3,2,1,0:T(8,128)(2,1)S(1)}, bf16[1,1,32,512]{3,2,1,0:T(8,128)(2,1)S(1)}, u32[]{:S(2)}, u32[]{:S(2)}) collective-permute-start(bf16[1,1,32,512]{3,2,1,0:T(8,128)(2,1)S(1)} %fusion.84), channel_id=1, source_target_pairs={{8,0},{16,8},{24,16},{0,24},{9,1},{17,9},{25,17},{1,25},{10,2},{18... | collective-permute-start | bytes 98312 | tf_op jit(solution)/shard_map/ppermute | solution.py:26
  49.9 57.3 %copy-start.3 = (bf16[2,128,128]{2,1,0:T(8,128)(2,1)S(1)}, bf16[2,128,128]{2,1,0:T(8,128)(2,1)}, u32[]{:S(2)}) copy-start(bf16[2,128,128]{2,1,0:T(8,128)(2,1)} %param.43) | copy-start | bytes 196612
  106.6 0.6 copy-start.8
  107.8 181.4 %collective-permute-start.6 = (bf16[3,1,32,512]{3,2,1,0:T(8,128)(2,1)S(1)}, bf16[3,1,32,512]{3,2,1,0:T(8,128)(2,1)}, u32[]{:S(2)}, u32[]{:S(2)}) collective-permute-start(bf16[3,1,32,512]{3,2,1,0:T(8,128)(2,1)S(1)} %pad_maximum_fusion.3), channel_id=1, source_target_pairs={{0,1},{1,2},{2,3},{3,4},{4,5},{5,6},{6,7},{7,0},{8,9},{9,10},{10,1... | collective-permute-start | bytes 294920 | tf_op jit(solution)/shard_map/ppermute | solution.py:25
  107.9 182.1 %collective-permute-start.7 = (bf16[3,1,32,512]{3,2,1,0:T(8,128)(2,1)S(1)}, bf16[3,1,32,512]{3,2,1,0:T(8,128)(2,1)}, u32[]{:S(2)}, u32[]{:S(2)}) collective-permute-start(bf16[3,1,32,512]{3,2,1,0:T(8,128)(2,1)S(1)} %pad_maximum_fusion.3), channel_id=1, source_target_pairs={{1,0},{2,1},{3,2},{4,3},{5,4},{6,5},{7,6},{0,7},{9,8},{10,9},{11,1... | collective-permute-start | bytes 294920 | tf_op jit(solution)/shard_map/ppermute | solution.py:26
  233.5 57.4 %copy-start.4 = (bf16[2,128,128]{2,1,0:T(8,128)(2,1)S(1)}, bf16[2,128,128]{2,1,0:T(8,128)(2,1)}, u32[]{:S(2)}) copy-start(bf16[2,128,128]{2,1,0:T(8,128)(2,1)} %param.40) | copy-start | bytes 196612
  288.4 3.3 copy-start.9
  288.4 3.3 copy-start.21
  288.4 3.3 copy-start.22
  288.4 3.3 copy-start.24
  291.7 71.1 %copy-start.5 = (bf16[2,128,128]{2,1,0:T(8,128)(2,1)S(1)}, bf16[2,128,128]{2,1,0:T(8,128)(2,1)}, u32[]{:S(2)}) copy-start(bf16[2,128,128]{2,1,0:T(8,128)(2,1)} %param.42) | copy-start | bytes 196612
  303.7 2.4 copy-start.1
  321.4 2.4 copy-start.1
  339.0 2.4 copy-start.1
  356.7 2.4 copy-start.1
  362.6 0.8 copy-start.10
  362.7 1.4 copy-start.11
  362.7 1.9 copy-start.12
  362.7 2.0 copy-start.25
  362.8 2.0 copy-start.28
  362.8 2.0 copy-start.29
  362.9 2.0 copy-start.30
  362.9 6.6 %copy-start.20 = (pred[2]{0:T(512)(128)(4,1)S(1)}, pred[2]{0:T(512)(128)(4,1)}, u32[]{:S(2)}) copy-start(pred[2]{0:T(512)(128)(4,1)} %copy-done.19) | copy-start | bytes 10
  362.9 6.6 %copy-start.26 = (s32[2]{0:T(128)S(1)}, s32[2]{0:T(128)}, u32[]{:S(2)}) copy-start(s32[2]{0:T(128)} %param.32) | copy-start | bytes 28
  363.0 11.2 %copy-start.13 = (s32[2]{0:T(128)S(1)}, s32[2]{0:T(128)}, u32[]{:S(2)}) copy-start(s32[2]{0:T(128)} %param.31) | copy-start | bytes 28
  363.0 11.1 %copy-start.15 = (pred[2]{0:T(512)(128)(4,1)S(1)}, pred[2]{0:T(512)(128)(4,1)}, u32[]{:S(2)}) copy-start(pred[2]{0:T(512)(128)(4,1)} %copy-done.14) | copy-start | bytes 10
  365.8 8.4 %all-to-all-start.2 = ((f32[8,4,128]{2,1,0:T(4,128)}), f32[8,4,128]{2,1,0:T(4,128)S(1)}, u32[]{:S(2)}, u32[]{:S(2)}) async-start(f32[8,4,128]{2,1,0:T(4,128)} %copy.79), calls=%async_computation.2 | async-start | bytes 32768 | tf_op jit(solution)/shard_map/all_to_all | solution.py:387
Sparse Core Ops, SparseCore 0:
  107.9 124.3 all-reduce.2
where the time goes:
time: 384 us; the launch traced here: 382 us
  matrix products  152 us (40%)
  waiting for transfers between devices  132 us (34%)
  local copies, waits for them, and re-layouts  29 us (8%)
  starting transfers between devices  26.1 us (7%)
  other arithmetic  22 us (6%)
  between operations  14.7 us (4%)
  loops' own time  6.29 us (2%)
    psum x1, waiting for transfers between devices, on_device(): total_real, total_imag = lax.psum((part_real, part_imag), ('gx', 'yz'))  122 us
    dot_general x8, matrix products, accumulate(): return running + jnp.dot(jnp.sin(phases), sin_right, precision=highest)  24.7 us
    dot_general x8, matrix products, accumulate(): running = running + jnp.dot(jnp.cos(phases), cos_right, precision=highest)  24.5 us
    dot_general x8, matrix products, one_block(): jnp.einsum('ak,aq->kq', jnp.sin(phases), charges, precision=highest)  23.1 us
    dot_general x8, matrix products, one_block(): jnp.einsum('ak,aq->kq', jnp.cos(phases), charges, precision=highest)  22.9 us
    dot_general x4, matrix products, edge_products(): jnp.dot(hidden, radial_out, preferred_element_type=jnp.float32)  18.3 us
    reduce_sum x4, other arithmetic, neighbour_sum(): jnp.sum(values.reshape(atom_count, slot_count, channels), axis=1)  13.6 us
    dot_general x4, matrix products, edge_products(): jnp.dot(row_onehot.astype(jnp.float32), table_pos.T, precision=highest)  12.4 us
  transfers between devices with their start and end apart: 12, of which 3 were waited for; matrix products, arithmetic and copies ran while one was open for 31% of the time, Pallas kernels for 0%

commit v1 on v0

v1 whole, which is shorter than its diff:
```python
import functools
import math

import jax
import jax.numpy as jnp
from jax import lax
from jax.experimental import pallas as pl
from jax.experimental.pallas import tpu as pltpu
from jax.sharding import PartitionSpec as P

highest = lax.Precision.HIGHEST
two_pi = 2.0 * math.pi
cutoff_radius = 3.5
basis_sharpness = 4.0
ewald_width = 0.1
ewald_scale = 0.01
z_reach = 2
lanes = 128
f32 = jnp.float32
bf16 = jnp.bfloat16

VMEM = pl.BlockSpec(memory_space=pltpu.VMEM)
SMEM = pl.BlockSpec(memory_space=pltpu.SMEM)
NT = (((1,), (1,)), ((), ()))
TN = (((0,), (0,)), ((), ()))


def nt(a, b, precision=None):
    return lax.dot_general(a, b, NT, precision=precision, preferred_element_type=f32)


def tn(a, b, precision=None):
    return lax.dot_general(a, b, TN, precision=precision, preferred_element_type=f32)


def mm(a, b, precision=None):
    return jnp.dot(a, b, precision=precision, preferred_element_type=f32)


def iota(shape, dim):
    return lax.broadcasted_iota(jnp.int32, shape, dim)


def silu(v):
    half = 0.5 * v
    return half + half * jnp.tanh(half)


def turn_cos_sin(turns):
    frac = turns - jnp.floor(turns + 0.5)
    angle = two_pi * frac
    return jnp.cos(angle), jnp.sin(angle)


def send_kernel(dest, slot, feat, pos, species, out):
    peers, block, _ = out.shape
    atoms, width = feat.shape
    blocks = atoms // block
    rows = jnp.concatenate(
        [pos[...].astype(f32), species[...].astype(f32), jnp.zeros((lanes - 4, atoms), f32)], axis=0
    )
    cols = rows.T
    lane = iota((block, lanes), 1)
    for d in range(peers):
        total = jnp.zeros((block, width), f32)
        side = jnp.zeros((block, lanes), f32)
        for b in range(blocks):
            chosen = jnp.where(dest[b] == d, 1.0, 0.0).astype(f32)
            total = total + chosen * feat[b * block : (b + 1) * block, :].astype(f32)
            mark = (slot[b] + 1).astype(f32)
            part = jnp.where(lane == 4, mark, cols[b * block : (b + 1) * block, :])
            side = side + chosen * part
        out[d, :, :width] = total.astype(bf16)
        out[d, :, width:] = side.astype(bf16)


def arrive_kernel(recv, halo, work, send, codes):
    peers, block, full = recv.shape
    atoms = work.shape[0]
    blocks = atoms // block
    width = full - lanes
    for s in range(blocks):
        total = jnp.zeros((block, full), f32)
        for d in range(peers):
            mark = recv[d, :, width + 4 : width + 5].astype(f32)
            total = total + jnp.where(mark == s + 1.0, 1.0, 0.0) * recv[d].astype(f32)
        work[s * block : (s + 1) * block, :] = total.astype(bf16)
    for d in range(peers):
        codes[d : d + 1, :] = jnp.broadcast_to(
            recv[d, 0:1, width + 4 : width + 5].astype(f32), (1, lanes)
        )
    count = halo.shape[0]
    pick = (halo[...] == iota((count, atoms), 1)).astype(f32).astype(bf16)
    send[...] = mm(pick, work[...]).astype(bf16)


def xz_factors(x_turns, z_turns, nx):
    steps = (iota((nx, x_turns.shape[1]), 0) + 1).astype(f32)
    xc, xs = turn_cos_sin(steps * x_turns)
    cos_rows, sin_rows = [], []
    for m in range(-z_reach, z_reach + 1):
        zc, zs = turn_cos_sin(m * z_turns)
        cos_rows.append(xc * zc - xs * zs)
        sin_rows.append(xc * zs + xs * zc)
    return jnp.concatenate(cos_rows, axis=0), jnp.concatenate(sin_rows, axis=0)


def wave_kernel(gx, yz, nyp, place, work, charge_t, partial, phases, charges):
    atoms, full = work.shape
    channels = charge_t.shape[1]
    pos = work[:, full - lanes :].astype(f32).T
    x_turns = (pos[0:1] + place[0]) * (1.0 / gx)
    y_turns = (pos[1:2] + place[1]) * (1.0 / yz)
    nx = 2 * gx
    xzc, xzs = xz_factors(x_turns, pos[2:3], nx)
    yc, ys = turn_cos_sin(iota((nyp, atoms), 0).astype(f32) * y_turns)
    q = nt(charge_t[...], work[:, :channels])
    pairs, latent = xzc.shape[0], q.shape[0]
    real = (xzc[:, None, :] * q[None]).reshape(pairs * latent, atoms)
    imag = (xzs[:, None, :] * q[None]).reshape(pairs * latent, atoms)
    ycs = jnp.concatenate([yc, ys], axis=0)
    partial[: 2 * nyp, :] = nt(ycs, real, highest)
    partial[2 * nyp :, :] = nt(ycs, imag, highest)
    phases[: 2 * nyp, :] = ycs
    phases[2 * nyp : 2 * nyp + pairs, :] = xzc
    phases[2 * nyp + pairs :, :] = xzs
    charges[...] = q


def grid_kernel(gx, yz, nyp, latent, wave, out):
    nx = 2 * gx
    cols = out.shape[1]
    count = wave.shape[1]
    group = iota((cols, count), 0) // latent
    code = (wave[2:3, :] + z_reach) * nx + wave[0:1, :] - 1
    hot = (group == code).astype(f32).astype(bf16)
    row = iota((nyp, count), 0)
    plus = (row == wave[1:2, :]).astype(f32).astype(bf16)
    minus = ((row == -wave[1:2, :]) & (row > 0)).astype(f32).astype(bf16)
    times = nt(jnp.concatenate([plus, minus], axis=0), hot)
    ny = (iota((2 * nyp, cols), 0) % nyp).astype(f32)
    pair = iota((2 * nyp, cols), 1) // latent
    wx = ((pair % nx) + 1).astype(f32) * (two_pi / gx)
    wz = ((pair // nx) - z_reach).astype(f32) * two_pi
    wy = ny * (two_pi / yz)
    squared = wx * wx + wy * wy + wz * wz
    prefactor = 8.0 * math.pi * ewald_scale / (gx * yz)
    out[...] = times * (prefactor * jnp.exp(-0.5 * ewald_width * ewald_width * squared) / squared)


def table_kernel(work, g0, g1, g2, g3, up, table_up, table_pos):
    full = work.shape[1]
    width = full - lanes
    channels = up.shape[1]
    feat = jnp.concatenate([r[...] for r in (work, g0, g1, g2, g3)], axis=0)
    for part in range(4):
        table_up[:, part * channels : (part + 1) * channels] = mm(
            feat[:, part * channels : (part + 1) * channels], up[min(part, 1)]
        ).astype(bf16)
    lane = iota((1, lanes), 1)
    sides = [work[:, width:].astype(f32)]
    for ref, axis, shift in ((g0, 0, -1.0), (g1, 0, 1.0), (g2, 1, -1.0), (g3, 1, 1.0)):
        sides.append(ref[:, width:].astype(f32) + jnp.where(lane == axis, shift, 0.0))
    pos = jnp.concatenate(sides, axis=0).T[:8]
    high = pos.astype(bf16)
    low = (pos - high.astype(f32)).astype(bf16)
    table_pos[...] = jnp.concatenate([high.astype(f32), low.astype(f32)], axis=0).astype(bf16)


def edge_kernel(
    slots, table_up, table_pos, nbr, centre, side, prod, rin_t, mid_t, rout, products
):
    table = table_up.shape[0]
    atoms = side.shape[0]
    channels = products.shape[1] // 4
    edges = atoms * slots
    row = nbr[0]
    hot_t = (iota((table, edges), 0) == row).astype(f32).astype(bf16)
    spread = (iota((atoms, edges), 0) == iota((atoms, edges), 1) // slots).astype(f32).astype(bf16)
    both = mm(table_pos[...], hot_t)
    own = mm(centre[0], spread)
    r = both[:8] + both[8:] - own[:8]
    dist = jnp.sqrt(r[0:1] * r[0:1] + r[1:2] * r[1:2] + r[2:3] * r[2:3])
    u = dist * (1.0 / cutoff_radius)
    u2 = u * u
    u6 = u2 * u2 * u2
    env = 1.0 + u6 * (-28.0 + u * (48.0 - 21.0 * u))
    live = (iota((1, edges), 1) % slots).astype(f32) < own[4:5]
    env = jnp.where(live, env, 0.0)
    nrad = 8
    centres = iota((2 * nrad, edges), 0).astype(f32) * (cutoff_radius / (nrad - 1))
    off = dist - centres
    basis = jnp.exp(-basis_sharpness * off * off).astype(bf16)
    h = silu(mm(rin_t[...], basis)).astype(bf16)
    h = silu(mm(mid_t[0], h)).astype(bf16)
    h = silu(mm(mid_t[1], h)) * env
    cols = jnp.concatenate(
        [h, r[:3], row.astype(f32), jnp.zeros((lanes - h.shape[0] - 4, edges), f32)], axis=0
    ).T
    base = h.shape[0]
    hot = (iota((edges, table), 1).astype(f32) == cols[:, base + 3 : base + 4]).astype(f32)
    up = mm(hot.astype(bf16), table_up[...])
    radial = mm(cols[:, :base].astype(bf16), rout[...])

    def part(source, k):
        return source[:, k * channels : (k + 1) * channels]

    rm = [cols[:, base + m : base + m + 1] for m in range(3)]
    u1 = [part(up, 1 + m) for m in range(3)]
    along = rm[0] * u1[0] + rm[1] * u1[1] + rm[2] * u1[2]

    def total(v):
        return jnp.sum(v.reshape(atoms, slots, channels), axis=1) * (1.0 / math.sqrt(slots))

    a0 = total(part(radial, 0) * part(up, 0) + part(radial, 1) * along)
    ru = part(radial, 2) * part(up, 0)
    rd = part(radial, 3)
    a1 = [total(ru * rm[m] + rd * u1[m]) for m in range(3)]
    kind = side[:, 3:4].astype(f32)
    p = jnp.zeros((atoms, prod.shape[1]), f32)
    for s in range(prod.shape[0]):
        p = p + jnp.where(kind == float(s), prod[s : s + 1, :], 0.0)
    square = a1[0] * a1[0] + a1[1] * a1[1] + a1[2] * a1[2]
    b0 = part(p, 0) * a0 + part(p, 1) * a0 * a0 + part(p, 2) * square
    products[:, :channels] = b0.astype(bf16)
    for m in range(3):
        products[:, (1 + m) * channels : (2 + m) * channels] = (
            part(p, 3) * a1[m] + part(p, 4) * a0 * a1[m]
        ).astype(bf16)


def final_kernel(
    gx, yz, nyp, sums, grid, phases, charges, products, work, ow, sw, fieldw, read_t, rvec, fw,
    codes, out,
):
    channels = ow.shape[1]
    atoms = work.shape[0]
    total = sums[0]
    for d in range(1, sums.shape[0]):
        total = total + sums[d]
    cre, sre, cim, sim = [total[k * nyp : (k + 1) * nyp] for k in range(4)]
    gp, gm = grid[:nyp], grid[nyp:]
    pre, pim = gp * (cre - sim), gp * (cim + sre)
    mre, mim = gm * (cre + sim), gm * (cim - sre)
    sum_re, sum_im, dif_re, dif_im = pre + mre, pim + mim, pre - mre, pim - mim
    wy = iota(sum_re.shape, 0).astype(f32) * (two_pi / yz)
    ycs = phases[: 2 * nyp, :]
    q = charges[...]
    latent = q.shape[0]
    pairs = sum_re.shape[1] // latent

    def contract(first, second):
        left = jnp.concatenate([first, second], axis=0)
        return tn(left, ycs, highest).reshape(pairs, latent, atoms)

    v_re = contract(sum_re, dif_im)
    v_im = contract(sum_im, -dif_re)
    y_re = contract(wy * dif_re, wy * sum_im)
    y_im = contract(wy * dif_im, -wy * sum_re)
    xzc = phases[2 * nyp : 2 * nyp + pairs, :][:, None, :]
    xzs = phases[2 * nyp + pairs :, :][:, None, :]
    d_re = xzc * v_re + xzs * v_im
    d_im = xzc * v_im - xzs * v_re
    d_y = xzc * y_im - xzs * y_re
    nx = 2 * gx
    pair = iota((pairs, latent, atoms), 0)
    wx = ((pair % nx) + 1).astype(f32) * (two_pi / gx)
    wz = ((pair // nx) - z_reach).astype(f32) * two_pi
    potential = jnp.sum(d_re, axis=0)
    efield = [-jnp.sum(wx * d_im, axis=0), -jnp.sum(d_y, axis=0), -jnp.sum(wz * d_im, axis=0)]
    scal = (
        mm(products[:, :channels], ow[0])
        + mm(work[:, :channels], sw[0])
        + tn(potential, fieldw[...], highest)
    )
    readout = silu(nt(read_t[...], scal.astype(bf16)))
    energy = jnp.sum(readout * rvec[...], axis=0, keepdims=True) + 0.5 * jnp.sum(
        q * potential, axis=0, keepdims=True
    )
    rows = []
    for m in range(3):
        cut = slice((1 + m) * channels, (2 + m) * channels)
        vec = mm(products[:, cut], ow[1]) + mm(work[:, cut], sw[1])
        rows.append(
            nt(fw[...], vec, highest)[0:1] + jnp.sum(q * efield[m], axis=0, keepdims=True)
        )
    rows.append(energy)
    result = jnp.concatenate(rows + [jnp.zeros((4, atoms), f32)], axis=0)
    peers, _, block = out.shape
    for d in range(peers):
        mark = codes[d : d + 1, :block]
        acc = jnp.zeros((8, block), f32)
        for s in range(atoms // block):
            acc = acc + jnp.where(mark == s + 1.0, result[:, s * block : (s + 1) * block], 0.0)
        out[d] = acc


def home_kernel(dest, came, forces, energies):
    block = came.shape[2]
    for b in range(forces.shape[1] // block):
        got = came[dest[b]]
        forces[:, b * block : (b + 1) * block] = got[:3]
        energies[:, b * block : (b + 1) * block] = got[3:4]


def call(body, specs, out_shape, *args, **kwargs):
    many = isinstance(out_shape, (list, tuple))
    return pl.pallas_call(
        body,
        out_shape=out_shape,
        in_specs=specs,
        out_specs=[VMEM] * len(out_shape) if many else VMEM,
        **kwargs,
    )(*args)


def shape(dims, dtype):
    return jax.ShapeDtypeStruct(tuple(dims), dtype)


def on_device(
    positions,
    species,
    features,
    move_dest,
    move_slot,
    halo_list,
    neighbours,
    neighbour_count,
    wave_index,
    radial_in,
    radial_mid,
    radial_out,
    up_weight,
    prod_weight,
    out_weight,
    skip_weight,
    charge_weight,
    field_weight,
    read_weight,
    read_vector,
    force_weight,
):
    gx, yz = lax.axis_size("gx"), lax.axis_size("yz")
    atoms, width = features.shape
    blocks = move_dest.shape[0]
    block = atoms // blocks
    slots = neighbours.shape[1]
    full = width + lanes
    latent = charge_weight.shape[1]
    nyp = -(-(2 * yz + 1) // 8) * 8
    nx = 2 * gx
    pairs = nx * (2 * z_reach + 1)
    cols = pairs * latent
    halo = halo_list.shape[0]

    outgoing = call(
        send_kernel,
        [SMEM, SMEM, VMEM, VMEM, VMEM],
        shape((yz, block, full), bf16),
        move_dest,
        move_slot,
        features,
        positions,
        species.reshape(1, atoms),
    )
    recv = lax.all_to_all(outgoing, "yz", split_axis=0, concat_axis=0, tiled=True)
    work, send, codes = call(
        arrive_kernel,
        [VMEM, VMEM],
        [shape((atoms, full), bf16), shape((halo, full), bf16), shape((yz, lanes), f32)],
        recv,
        halo_list.reshape(halo, 1),
    )

    def ring(axis, step):
        count = lax.axis_size(axis)
        return lax.ppermute(send, axis, [(i, (i + step) % count) for i in range(count)])

    ghosts = [ring("gx", 1), ring("gx", -1), ring("yz", 1), ring("yz", -1)]
    grid = call(
        functools.partial(grid_kernel, gx, yz, nyp, latent),
        [VMEM],
        shape((2 * nyp, cols), f32),
        wave_index,
    )
    place = jnp.stack([lax.axis_index("gx"), lax.axis_index("yz")]).astype(f32)
    partial, phases, charges = call(
        functools.partial(wave_kernel, gx, yz, nyp),
        [SMEM, VMEM, VMEM],
        [
            shape((4 * nyp, cols), f32),
            shape((2 * nyp + 2 * pairs, atoms), f32),
            shape((latent, atoms), f32),
        ],
        place,
        work,
        charge_weight.T,
    )
    row_sums = jnp.sum(lax.all_gather(partial, "gx"), axis=0)
    sums = lax.all_gather(row_sums, "yz")
    table = atoms + 4 * halo
    table_up, table_pos = call(
        table_kernel,
        [VMEM] * 6,
        [shape((table, width), bf16), shape((16, table), bf16)],
        work,
        *ghosts,
        up_weight,
    )
    step = math.gcd(atoms, 32)
    steps = atoms // step
    edges = step * slots
    side = work[:, width:]
    own = jnp.concatenate([side[:, :4].T, neighbour_count.astype(bf16)[None]], axis=0)
    own = jnp.pad(own, ((0, 11), (0, 0))).reshape(16, steps, step).transpose(1, 0, 2)
    hidden = radial_mid.shape[1]
    nrad = radial_in.shape[0]
    rin_t = jnp.pad(radial_in.T, ((0, 0), (0, 16 - nrad)))

    def whole(a):
        return pl.BlockSpec(a.shape, lambda i: (0,) * a.ndim)

    mid_t = radial_mid.transpose(0, 2, 1)
    products = pl.pallas_call(
        functools.partial(edge_kernel, slots),
        out_shape=shape((atoms, width), bf16),
        grid=(steps,),
        in_specs=[
            whole(table_up),
            whole(table_pos),
            pl.BlockSpec((1, 1, edges), lambda i: (i, 0, 0)),
            pl.BlockSpec((1, 16, step), lambda i: (i, 0, 0)),
            pl.BlockSpec((step, lanes), lambda i: (i, 0)),
            whole(prod_weight),
            whole(rin_t),
            whole(mid_t),
            whole(radial_out),
        ],
        out_specs=pl.BlockSpec((step, width), lambda i: (i, 0)),
        compiler_params=pltpu.CompilerParams(vmem_limit_bytes=56 * 1024 * 1024),
    )(
        table_up,
        table_pos,
        neighbours.reshape(steps, 1, edges),
        own,
        side,
        prod_weight,
        rin_t,
        mid_t,
        radial_out,
    )
    back = call(
        functools.partial(final_kernel, gx, yz, nyp),
        [VMEM] * 13,
        shape((yz, 8, block), f32),
        sums,
        grid,
        phases,
        charges,
        products,
        work,
        out_weight,
        skip_weight,
        field_weight,
        read_weight.T,
        read_vector.reshape(-1, 1),
        jnp.broadcast_to(force_weight[None], (8, force_weight.shape[0])),
        codes,
    )
    came = lax.all_to_all(back, "yz", split_axis=0, concat_axis=0, tiled=True)
    forces, energies = call(
        home_kernel,
        [SMEM, VMEM],
        [shape((3, atoms), f32), shape((1, atoms), f32)],
        move_dest,
        came,
    )
    return (forces, energies.reshape(atoms))


def solution(mesh):
    split = P(("gx", "yz"))
    rows = P(("gx", "yz"), None)
    in_specs = (P(None, ("gx", "yz")), split, rows, split, split, split, rows, split) + (P(),) * 13
    out_specs = (P(None, ("gx", "yz")), split)
    return jax.shard_map(
        on_device, mesh=mesh, in_specs=in_specs, out_specs=out_specs, check_vma=False
    )
```

time: 384 us -> 121 us (0.32)
  matrix products: 152 us -> 0 us
  waiting for transfers between devices: 132 us -> 11.5 us
  Pallas kernels: 0 us -> 48.9 us
  blocking collectives: 0 us -> 36.6 us
  other arithmetic: 22 us -> 0.7 us
  local copies, waits for them, and re-layouts: 29 us -> 9.67 us
  starting transfers between devices: 26.1 us -> 11.8 us
  between operations: 14.7 us -> 0.74 us
  loops' own time: 6.29 us -> 0 us
    dot_general x73 -> x0, matrix products: 152 us -> none  [the longest x8 24.7 us: accumulate(): return running + jnp.dot(jnp.sin(phases), sin_right, precision=highest)]
    psum x1 -> x0, waiting for transfers between devices: 122 us -> none  [on_device(): total_real, total_imag = lax.psum((part_real, part_imag), ('gx', 'yz'))]
    pallas_call x0 -> x8, Pallas kernels: none -> 48.9 us  [the longest x1 30.3 us: on_device(): pl.pallas_call(functools.partial(edge_kernel, slots), out_shape=shape((at...]
    all_gather x0 -> x2, blocking collectives: none -> 27.8 us  [the longest x1 16.5 us: on_device(): row_sums = jnp.sum(lax.all_gather(partial, 'gx'), axis=0)]
    reduce_sum x6 -> x1, other arithmetic: 14.4 us -> 0.03 us  [on_device(): row_sums = jnp.sum(lax.all_gather(partial, 'gx'), axis=0)]
    all_to_all x0 -> x1, blocking collectives: none -> 8.77 us  [on_device(): came = lax.all_to_all(back, 'yz', split_axis=0, concat_axis=0, tiled=True)]
    all_to_all x3 -> x1, starting transfers between devices: 13 us -> 5.34 us  [on_device(): lax.all_to_all(outgoing, 'yz', split_axis=0, concat_axis=0, tiled=True)]
    all_to_all x3 -> x1, waiting for transfers between devices: 4.55 us -> 11.5 us  [on_device(): lax.all_to_all(outgoing, 'yz', split_axis=0, concat_axis=0, tiled=True)]
  transfers between devices with their start and end apart: 12 -> 5, of which waited for: 3 -> 1; matrix products, arithmetic and copies ran while one was open for 31% -> 6% of each run, Pallas kernels for 0% -> 4%
where the time goes in v1:
time: 121 us; the launch traced here: 120 us
  Pallas kernels  48.9 us (40%)
  blocking collectives  36.6 us (30%)
  starting transfers between devices  11.8 us (10%)
  waiting for transfers between devices  11.5 us (10%)
  local copies, waits for them, and re-layouts  9.67 us (8%)
    pallas_call x1, Pallas kernels, on_device(): pl.pallas_call(functools.partial(edge_kernel, slots), out_shape=shape((at...  30.3 us
    pallas_call x7, Pallas kernels, call(): pl.pallas_call(body, out_shape=out_shape, in_specs=specs, out_specs=[VMEM...  18.6 us
    all_gather x1, blocking collectives, on_device(): row_sums = jnp.sum(lax.all_gather(partial, 'gx'), axis=0)  16.5 us
    all_to_all x1, waiting for transfers between devices, on_device(): lax.all_to_all(outgoing, 'yz', split_axis=0, concat_axis=0, tiled=True)  11.5 us
    all_gather x1, blocking collectives, on_device(): sums = lax.all_gather(row_sums, 'yz')  11.3 us
    all_to_all x1, blocking collectives, on_device(): came = lax.all_to_all(back, 'yz', split_axis=0, concat_axis=0, tiled=True)  8.77 us
    ppermute x4, starting transfers between devices, ring(): lax.ppermute(send, axis, [(i, (i + step) % count) for i in range(count)])  6.47 us
    all_to_all x1, starting transfers between devices, on_device(): lax.all_to_all(outgoing, 'yz', split_axis=0, concat_axis=0, tiled=True)  5.34 us
  transfers between devices with their start and end apart: 5, of which 1 were waited for; matrix products, arithmetic and copies ran while one was open for 6% of the time, Pallas kernels for 4%

profile of v1, /device:TPU:0, one launch (start us, length us, event | category | flops | bytes accessed | tf_op | source)
XLA Modules:
  0.0 119.9 jit_solution(17211583993821936482)
XLA Ops:
  0.6 2.7 %shard_map.212 = bf16[8,128,640]{2,1,0:T(8,128)(2,1)} custom-call(s32[2]{0:T(128)} %dest.3, s32[2]{0:T(128)} %slot.1, bf16[256,512]{1,0:T(8,128)(2,1)} %feat.1, bf16[3,256]{1,0:T(4,128)(2,1)} %pos.1, s32[1,256]{1,0:T(1,128)} %bitcast.24), custom_call_target="tpu_custom_call" | custom-call | tf_op jit(solution)/shard_map/pallas_call | solution.py:308
  3.3 0.0 copy-start.6
  3.4 0.0 copy-start.7
  3.4 0.0 copy-start.9
  3.4 5.3 %all-to-all-start = ((bf16[8,128,640]{2,1,0:T(8,128)(2,1)}), bf16[8,128,640]{2,1,0:T(8,128)(2,1)S(1)}, u32[]{:S(2)}, u32[]{:S(2)}) async-start(bf16[8,128,640]{2,1,0:T(8,128)(2,1)} %shard_map.212), calls=%async_computation | async-start | bytes 2621440 | tf_op jit(solution)/shard_map/all_to_all | solution.py:367
  8.7 0.0 copy-done.8
  8.7 0.7 copy.37.halo
  9.4 0.0 copy-done.11
  9.4 0.0 copy-done.1
  9.4 0.1 copy.38
  9.5 0.8 reshape.31.nbr
  10.3 0.7 copy.42
  11.0 0.1 copy.41
  11.1 2.3 %shard_map.215.grid = f32[48,320]{1,0:T(8,128)} custom-call(s32[3,4096]{1,0:T(4,128)} %wave.1), custom_call_target="tpu_custom_call" | custom-call | tf_op jit(solution)/shard_map/pallas_call | solution.py:308
  13.4 0.7 copy.44.rvec
  14.1 0.6 pad.9.rin_t
  14.7 0.6 add_convert_fusion.place
  15.4 11.5 %all-to-all-done.recv = bf16[8,128,640]{2,1,0:T(8,128)(2,1)S(1)} async-done(((bf16[8,128,640]{2,1,0:T(8,128)(2,1)}), bf16[8,128,640]{2,1,0:T(8,128)(2,1)S(1)}, u32[]{:S(2)}, u32[]{:S(2)}) %all-to-all-start) | async-done | bytes 1310752 | tf_op jit(solution)/shard_map/all_to_all | solution.py:367
  26.9 1.1 copy-done
  28.0 2.8 %shard_map.213 = (bf16[256,640]{1,0:T(8,128)(2,1)}, bf16[32,640]{1,0:T(8,128)(2,1)}, f32[8,128]{1,0:T(8,128)}) custom-call(bf16[8,128,640]{2,1,0:T(8,128)(2,1)} %copy-done, s32[32,1]{1,0:T(8,128)} %copy.37.halo), custom_call_target="tpu_custom_call" | custom-call | tf_op jit(solution)/shard_map/pallas_call | solution.py:308
  30.8 1.6 %collective-permute-start = (bf16[32,640]{1,0:T(8,128)(2,1)}, bf16[32,640]{1,0:T(8,128)(2,1)S(1)}, u32[]{:S(2)}, u32[]{:S(2)}) collective-permute-start(bf16[32,640]{1,0:T(8,128)(2,1)} %get-tuple-element.16), channel_id=1, source_target_pairs={{0,8},{8,16},{16,24},{24,0},{1,9},{9,17},{17,25},{25,1},{2,10},{10... | collective-permute-start | bytes 122888 | tf_op jit(solution)/shard_map/ppermute | solution.py:378
  32.3 2.2 %collective-permute-start.1 = (bf16[32,640]{1,0:T(8,128)(2,1)}, bf16[32,640]{1,0:T(8,128)(2,1)S(1)}, u32[]{:S(2)}, u32[]{:S(2)}) collective-permute-start(bf16[32,640]{1,0:T(8,128)(2,1)} %get-tuple-element.16), channel_id=1, source_target_pairs={{0,24},{8,0},{16,8},{24,16},{1,25},{9,1},{17,9},{25,17},{2,26},{10... | collective-permute-start | bytes 122888 | tf_op jit(solution)/shard_map/ppermute | solution.py:378
  34.6 0.0 collective-permute-start.2
  34.6 2.6 %collective-permute-start.3 = (bf16[32,640]{1,0:T(8,128)(2,1)}, bf16[32,640]{1,0:T(8,128)(2,1)S(1)}, u32[]{:S(2)}, u32[]{:S(2)}) collective-permute-start(bf16[32,640]{1,0:T(8,128)(2,1)} %get-tuple-element.16), channel_id=1, source_target_pairs={{0,7},{1,0},{2,1},{3,2},{4,3},{5,4},{6,5},{7,6},{8,15},{9,8},{10,9... | collective-permute-start | bytes 122888 | tf_op jit(solution)/shard_map/ppermute | solution.py:378
  37.2 0.8 slice_bitcast_fusion
  38.1 0.1 copy.39
  38.2 2.8 %shard_map.214 = (f32[96,320]{1,0:T(8,128)}, f32[128,256]{1,0:T(8,128)}, f32[8,256]{1,0:T(8,128)}) custom-call(f32[2]{0:T(128)} %add_convert_fusion.place, bf16[256,640]{1,0:T(8,128)(2,1)} %get-tuple-element.12.work, bf16[8,128]{1,0:T(8,128)(2,1)} %bitcast.23), custom_call_target="tpu_custom_call" | custom-call | tf_op jit(solution)/shard_map/pallas_call | solution.py:308
  40.9 16.5 %all-gather = f32[384,320]{1,0:T(8,128)S(1)} all-gather(f32[96,320]{1,0:T(8,128)} %get-tuple-element.13), channel_id=2, replica_groups=mesh['gx'=4,'yz'=8] {'gx'}, dimensions={0}, use_global_device_ids=true | all-gather | bytes 614400 | tf_op jit(solution)/shard_map/all_gather | solution.py:400
  57.4 0.0 copy-start.10
  57.4 11.3 %all-gather.1 = f32[768,320]{1,0:T(8,128)} all-gather(f32[96,320]{1,0:T(8,128)S(1)} %reduce_sum.9), channel_id=3, replica_groups=mesh['gx'=4,'yz'=8] {'yz'}, dimensions={0}, use_global_device_ids=true | all-gather | bytes 1105920 | tf_op jit(solution)/shard_map/all_gather | solution.py:401
  68.8 1.5 %slice.8.side = bf16[256,128]{1,0:T(8,128)(2,1)} slice(bf16[256,640]{1,0:T(8,128)(2,1)} %get-tuple-element.12.work), slice={[0:256], [512:640]} | slice | bytes 131072 | tf_op jit(solution)/shard_map/slice | solution.py:414
  70.2 0.1 reshape.26
  70.3 0.6 copy.46
  71.0 0.0 collective-permute-done.g0
  71.0 0.0 collective-permute-done.1.g1
  71.0 0.0 copy-start.3
  71.0 0.0 collective-permute-done.2.g2
  71.0 0.0 collective-permute-done.3.g3
  71.0 0.6 copy-done.2
  71.6 0.0 copy-done.3
  71.6 0.0 copy-done.4
  71.6 0.6 copy-done.5
  72.2 2.0 %shard_map.216 = (bf16[384,512]{1,0:T(8,128)(2,1)}, bf16[16,384]{1,0:T(8,128)(2,1)}) custom-call(bf16[256,640]{1,0:T(8,128)(2,1)} %get-tuple-element.12.work, bf16[32,640]{1,0:T(8,128)(2,1)} %copy-done.2, bf16[32,640]{1,0:T(8,128)(2,1)} %copy-done.3, bf16[32,640]{1,0:T(8,128)(2,1)} %copy-done.4, bf16[32,640]{1,0:T(8,128)(2,1)} %copy-done.5, ...), custom_call_target="tpu_custom_call" | custom-call | tf_op jit(solution)/shard_map/pallas_call | solution.py:308
  74.2 30.3 %shard_map.217.products = bf16[256,512]{1,0:T(8,128)(2,1)} custom-call(bf16[384,512]{1,0:T(8,128)(2,1)} %get-tuple-element.17.table_up, bf16[16,384]{1,0:T(8,128)(2,1)} %get-tuple-element.18.table_pos, s32[8,1,2048]{2,1,0:T(1,128)} %reshape.31.nbr, bf16[8,16,32]{2,1,0:T(8,128)(2,1)} %bitcast.20, bf16[256,128]{1,0:T(8,128)(2,1)} %slice.8.side, ...), custom_call_target="tpu_custom_call" | custom-call | tf_op jit(solution)/shard_map/pallas_call | solution.py:425
  104.5 0.6 broadcast_in_dim.10.fw
  105.1 4.6 %shard_map.218 = f32[8,8,128]{2,1,0:T(8,128)} custom-call(f32[8,96,320]{2,1,0:T(8,128)} %bitcast.17, f32[48,320]{1,0:T(8,128)} %shard_map.215.grid, f32[128,256]{1,0:T(8,128)} %get-tuple-element.14.phases, f32[8,256]{1,0:T(8,128)} %get-tuple-element.15.charges, bf16[256,512]{1,0:T(8,128)(2,1)} %shard_map.217.products, ...), custom_call_target="tpu_custom_call" | custom-call | tf_op jit(solution)/shard_map/pallas_call | solution.py:308
  109.7 8.8 %all_to_all.10.came = f32[8,8,128]{2,1,0:T(8,128)} all-to-all(f32[8,8,128]{2,1,0:T(8,128)} %shard_map.218), channel_id=1, replica_groups=mesh['gx'=4,'yz'=8] {'yz'}, dimensions={0} | all-to-all | bytes 65536 | tf_op jit(solution)/shard_map/all_to_all | solution.py:471
  118.5 1.4 %shard_map.219 = (f32[3,256]{1,0:T(4,128)}, f32[1,256]{1,0:T(1,128)}) custom-call(s32[2]{0:T(128)} %dest.3, f32[8,8,128]{2,1,0:T(8,128)} %all_to_all.10.came), custom_call_target="tpu_custom_call" | custom-call | tf_op jit(solution)/shard_map/pallas_call | solution.py:308
  (15 shorter events, 0.1 us)
Async XLA Ops:
  3.3 5.4 %copy-start.8 = (s32[32]{0:T(128)S(1)}, s32[32]{0:T(128)}, u32[]{:S(2)}) copy-start(s32[32]{0:T(128)} %param.26) | copy-start | bytes 388
  3.3 6.1 %copy-start.11 = (s32[256]{0:T(256)S(1)}, s32[256]{0:T(256)}, u32[]{:S(2)}) copy-start(s32[256]{0:T(256)} %param.28) | copy-start | bytes 3076
  3.3 6.1 %copy-start.1 = (s32[256,64]{0,1:T(8,128)S(1)}, s32[256,64]{0,1:T(8,128)}, u32[]{:S(2)}) copy-start(s32[256,64]{0,1:T(8,128)} %param.27) | copy-start | bytes 196612
  3.3 6.9 %copy-start.6 = (bf16[2,64,64]{2,1,0:T(8,128)(2,1)S(1)}, bf16[2,64,64]{2,1,0:T(8,128)(2,1)}, u32[]{:S(2)}) copy-start(bf16[2,64,64]{2,1,0:T(8,128)(2,1)} %param.31) | copy-start | bytes 49156
  3.4 7.6 %copy-start.7 = (bf16[8,64]{1,0:T(8,128)(2,1)S(1)}, bf16[8,64]{1,0:T(8,128)(2,1)}, u32[]{:S(2)}) copy-start(bf16[8,64]{1,0:T(8,128)(2,1)} %param.30) | copy-start | bytes 3076
  3.4 10.1 %copy-start.9 = (f32[16]{0:T(128)S(1)}, f32[16]{0:T(128)}, u32[]{:S(2)}) copy-start(f32[16]{0:T(128)} %param.40) | copy-start | bytes 196
  3.4 23.5 %all-to-all-start = ((bf16[8,128,640]{2,1,0:T(8,128)(2,1)}), bf16[8,128,640]{2,1,0:T(8,128)(2,1)S(1)}, u32[]{:S(2)}, u32[]{:S(2)}) async-start(bf16[8,128,640]{2,1,0:T(8,128)(2,1)} %shard_map.212), calls=%async_computation | async-start | bytes 2621440 | tf_op jit(solution)/shard_map/all_to_all | solution.py:367
  26.9 1.1 copy-start
  30.8 40.2 %collective-permute-start = (bf16[32,640]{1,0:T(8,128)(2,1)}, bf16[32,640]{1,0:T(8,128)(2,1)S(1)}, u32[]{:S(2)}, u32[]{:S(2)}) collective-permute-start(bf16[32,640]{1,0:T(8,128)(2,1)} %get-tuple-element.16), channel_id=1, source_target_pairs={{0,8},{8,16},{16,24},{24,0},{1,9},{9,17},{17,25},{25,1},{2,10},{10... | collective-permute-start | bytes 122888 | tf_op jit(solution)/shard_map/ppermute | solution.py:378
  32.3 38.6 %collective-permute-start.1 = (bf16[32,640]{1,0:T(8,128)(2,1)}, bf16[32,640]{1,0:T(8,128)(2,1)S(1)}, u32[]{:S(2)}, u32[]{:S(2)}) collective-permute-start(bf16[32,640]{1,0:T(8,128)(2,1)} %get-tuple-element.16), channel_id=1, source_target_pairs={{0,24},{8,0},{16,8},{24,16},{1,25},{9,1},{17,9},{25,17},{2,26},{10... | collective-permute-start | bytes 122888 | tf_op jit(solution)/shard_map/ppermute | solution.py:378
  34.6 36.4 %collective-permute-start.2 = (bf16[32,640]{1,0:T(8,128)(2,1)}, bf16[32,640]{1,0:T(8,128)(2,1)S(1)}, u32[]{:S(2)}, u32[]{:S(2)}) collective-permute-start(bf16[32,640]{1,0:T(8,128)(2,1)} %get-tuple-element.16), channel_id=1, source_target_pairs={{0,1},{1,2},{2,3},{3,4},{4,5},{5,6},{6,7},{7,0},{8,9},{9,10},{10,1... | collective-permute-start | bytes 122888 | tf_op jit(solution)/shard_map/ppermute | solution.py:378
  34.6 36.4 %collective-permute-start.3 = (bf16[32,640]{1,0:T(8,128)(2,1)}, bf16[32,640]{1,0:T(8,128)(2,1)S(1)}, u32[]{:S(2)}, u32[]{:S(2)}) collective-permute-start(bf16[32,640]{1,0:T(8,128)(2,1)} %get-tuple-element.16), channel_id=1, source_target_pairs={{0,7},{1,0},{2,1},{3,2},{4,3},{5,4},{6,5},{7,6},{8,15},{9,8},{10,9... | collective-permute-start | bytes 122888 | tf_op jit(solution)/shard_map/ppermute | solution.py:378
  57.4 47.1 %copy-start.10 = (f32[128]{0:T(128)S(1)}, f32[128]{0:T(128)}, u32[]{:S(2)}) copy-start(f32[128]{0:T(128)} %param.41) | copy-start | bytes 1540
  71.0 0.6 copy-start.2
  71.0 0.6 copy-start.3
  71.0 0.6 copy-start.4
  71.6 0.6 copy-start.5
